TPU v7x, 32 devices: a whole 2x2x4 slice. The times are simulated.
32 devices in a mesh: tm: 8 (over y, x, core), rows: 4 (over z).
Axes of the slice: x: 2, y: 2, z: 4, core: 2. Of those that a mesh axis runs over, the one named last changes fastest.
Arguments:
- frames_in: bfloat16 [32, 32, 32, 512], P('tm', 'rows'), may hold values from -6 to 6
- weight_in: bfloat16 [2, 512, 4608], P(None, 'rows'), may hold values from -0.09375 to 0.09375
- weight_out: bfloat16 [9, 2, 512, 512], P(None, None, 'rows'), may hold values from -0.015625 to 0.015625
- log_decay: float32 [512], replicated, may hold values from 0.0003125 to 0.06
- rotation: float32 [512], replicated, may hold values from -3.140625 to 3.140625
- start_state: float32 [32, 32, 2, 512], P('rows'), may hold values from -12 to 12
- skip_gain: float32 [512], replicated, may hold values from -1 to 1
Outputs:
- frames_out: bfloat16 [32, 32, 32, 512], P('tm', 'rows')
All inputs are finite; a program needn't handle non-finite values.
Results may differ from a plain program's by a relative error of at most 0.0047.
Values may be sent and summed in bfloat16 or wider, within the bound.
A program may use at most 128 MiB of HBM per device.

v0:
```python
import jax
import jax.numpy as jnp
from jax import lax
from jax.sharding import PartitionSpec as P


def passed_along(value, axis, steps):
    count = lax.axis_size(axis)
    first, last = (max(0, -steps), min(count, count - steps))
    return lax.ppermute(value, axis, [(source, source + steps) for source in range(first, last)])


def extended_2(cells, sides, width):
    for axis, dim in sides:
        count = lax.axis_size(axis)
        ends = count - 1
        head = lax.slice_in_dim(cells, 0, width, axis=dim)
        tail = lax.slice_in_dim(cells, cells.shape[dim] - width, cells.shape[dim], axis=dim)
        cells = jnp.concatenate(
            [
                lax.ppermute(tail, axis, [(i, (i + 1) % count) for i in range(ends)]),
                cells,
                lax.ppermute(head, axis, [((i + 1) % count, i) for i in range(ends)]),
            ],
            axis=dim,
        )
    return cells


def pad_field(field, rows_pad):
    widths = [(0, 0)] * field.ndim
    widths[1] = (rows_pad, rows_pad)
    widths[2] = (1, 1)
    return jnp.pad(field, widths)


def in_term(padded, piece, height, columns):
    parts, state_width, span = piece.shape
    channels = span // 9
    matrix = piece.reshape(parts * state_width, span)
    summed = jnp.zeros((padded.shape[0], height, columns, parts * state_width), jnp.float32)
    for tap_index in range(9):
        row_shift = tap_index // 3
        col_shift = tap_index % 3
        window = padded[:, row_shift : row_shift + height, col_shift : col_shift + columns, :]
        weight_tap = matrix[:, tap_index * channels : (tap_index + 1) * channels]
        summed = summed + lax.dot_general(
            window, weight_tap, (((3,), (1,)), ((), ())), preferred_element_type=jnp.float32
        )
    return summed.reshape(padded.shape[0], height, columns, parts, state_width)


def out_term(padded_held, piece, height, columns):
    summed = jnp.zeros((padded_held.shape[0], height, columns, piece.shape[3]), jnp.float32)
    for tap_index in range(9):
        row_shift = tap_index // 3
        col_shift = tap_index % 3
        window = padded_held[:, row_shift : row_shift + height, col_shift : col_shift + columns]
        summed = summed + lax.dot_general(
            window,
            piece[tap_index],
            (((3, 4), (0, 1)), ((), ())),
            preferred_element_type=jnp.float32,
        )
    return summed


def run_states(driven, start_re, start_im, log_rate, angle):
    frame_count = driven.shape[0]
    modulus = jnp.exp(-log_rate)
    lam_re = modulus * jnp.cos(angle)
    lam_im = modulus * jnp.sin(angle)
    is_first = lax.axis_index("tm") == 0
    begin_re = jnp.where(is_first, start_re, jnp.float32(0.0))
    begin_im = jnp.where(is_first, start_im, jnp.float32(0.0))

    def advance(carried, forcing):
        state_re, state_im = carried
        force_re, force_im = forcing
        new_re = lam_re * state_re - lam_im * state_im + force_re
        new_im = lam_re * state_im + lam_im * state_re + force_im
        return ((new_re, new_im), (new_re, new_im))

    (tail_re, tail_im), (local_re, local_im) = lax.scan(
        advance, (begin_re, begin_im), (driven[..., 0, :], driven[..., 1, :])
    )
    span_mod = jnp.exp(-log_rate * frame_count)
    span_re = span_mod * jnp.cos(angle * frame_count)
    span_im = span_mod * jnp.sin(angle * frame_count)

    def relay(turn_index, carried):
        prior_re, prior_im = carried
        sent_re = span_re * prior_re - span_im * prior_im + tail_re
        sent_im = span_re * prior_im + span_im * prior_re + tail_im
        return passed_along((sent_re, sent_im), "tm", 1)

    carry_re, carry_im = lax.fori_loop(
        0, lax.axis_size("tm") - 1, relay, (jnp.zeros_like(tail_re), jnp.zeros_like(tail_im))
    )
    step_count = jnp.arange(1, frame_count + 1, dtype=jnp.float32)[:, None, None, None]
    power_mod = jnp.exp(-log_rate * step_count)
    power_re = power_mod * jnp.cos(angle * step_count)
    power_im = power_mod * jnp.sin(angle * step_count)
    states_re = local_re + power_re * carry_re - power_im * carry_im
    states_im = local_im + power_re * carry_im + power_im * carry_re
    return jnp.stack([states_re, states_im], 3).astype(jnp.bfloat16)


def on_device(frames_in, weight_in, weight_out, log_decay, rotation, start_state, skip_gain):
    frame_count, band_rows, columns, channels = frames_in.shape
    extended = extended_2(frames_in, (("rows", 1),), 1)
    padded = pad_field(extended, 0)
    driven = in_term(
        padded, lax.all_gather(weight_in, "rows", axis=1, tiled=True), band_rows, columns
    )
    held = run_states(driven, start_state[:, :, 0, :], start_state[:, :, 1, :], log_decay, rotation)
    held = extended_2(held, (("rows", 1),), 1)
    held_padded = pad_field(held, 0)
    mixing = out_term(
        held_padded, lax.all_gather(weight_out, "rows", axis=2, tiled=True), band_rows, columns
    )
    pre_act = mixing + skip_gain * frames_in.astype(jnp.float32)
    return jax.nn.gelu(pre_act, approximate=False).astype(jnp.bfloat16)


def solution(mesh):
    return jax.shard_map(
        on_device,
        mesh=mesh,
        in_specs=(
            P("tm", "rows", None, None),
            P(None, "rows", None),
            P(None, None, "rows", None),
            P(),
            P(),
            P("rows", None, None, None),
            P(),
        ),
        out_specs=P("tm", "rows", None, None),
        check_vma=False,
    )
```

profile of v0, /device:TPU:12, one launch (start us, length us, event | category | flops | bytes accessed | tf_op | source)
XLA Modules:
  0.0 405.1 jit_solution(16774444298382258066)
XLA Ops:
  9.0 3.5 collective-permute-start.2
  12.5 2.4 collective-permute-start.3
  16.3 3.0 collective-permute-done.3
  20.2 153.8 %all-gather.3.cloned.1.call-done = bf16[2,512,4608]{2,1,0:T(8,128)(2,1)} async-done(((bf16[2,128,4608]{2,1,0:T(8,128)(2,1)}), bf16[2,512,4608]{2,1,0:T(8,128)(2,1)}) %all-gather.3.cloned.1.call-update) | async-done | bytes 9437200 | tf_op jit(solution)/shard_map/all_gather | solution.py:114
  174.1 2.9 fusion.51
  177.0 3.2 fusion.55
  180.2 3.3 fusion.63
  183.5 3.4 fusion.65
  186.8 3.3 fusion.68
  190.2 3.2 fusion.70
  193.4 3.2 fusion.72
  196.7 3.4 fusion.67
  200.0 11.9 %add_add_fusion.1 = f32[4,8,32,1024]{3,2,1,0:T(8,128)} fusion(f32[4,8,32,1024]{3,2,1,0:T(8,128)S(1)} %fusion.55, f32[4,8,32,1024]{3,2,1,0:T(8,128)} %fusion.63, f32[4,8,32,1024]{3,2,1,0:T(8,128)} %fusion.65, f32[4,8,32,1024]{3,2,1,0:T(8,128)} %fusion.67, f32[4,8,32,1024]{3,2,1,0:T(8,128)} %fusion.68, f32[4,8,32,1024]{3,2,1,0:T(8,128)} %fusion.70, ...), kind=kOutput, calls=%fused_computation.11 | convolution fusion | flops 1082130432 | bytes 39845888 | tf_op jit(solution)/shard_map/dot_general | solution.py:47
  211.9 6.6 %reshape.132 = f32[4,8,32,2,512]{4,3,2,1,0:T(2,128)} reshape(f32[4,8,32,1024]{3,2,1,0:T(8,128)} %add_add_fusion.1) | data formatting | bytes 8388608 | tf_op jit(solution)/shard_map/reshape | solution.py:50
  218.5 7.9 %fusion.83 = (f32[4,8,32,1,512]{4,3,2,1,0:T(1,128)S(1)}, f32[4,8,32,1,512]{4,3,2,1,0:T(1,128)S(1)}) fusion(f32[4,8,32,2,512]{4,3,2,1,0:T(2,128)} %reshape.132), kind=kLoop, calls=%fused_computation.146 | loop fusion | bytes 8388608 | tf_op jit(solution)/shard_map/slice | solution.py:85
  226.4 2.0 copy_bitcast_fusion
  228.3 1.7 broadcast.93
  230.0 1.6 broadcast.93.clone
  231.6 9.8 %while.28 = (s32[]{:T(128)}, f32[8,32,512]{2,1,0:T(8,128)S(1)}, f32[8,32,512]{2,1,0:T(8,128)S(1)}, f32[4,8,32,512]{3,2,1,0:T(8,128)}, f32[4,8,32,512]{3,2,1,0:T(...) while((s32[]{:T(128)}, f32[8,32,512]{2,1,0:T(8,128)S(1)}, ...), condition=%wide.region_1.2_spmd, body=%wide.region_0.1_spmd.sunk | while | flops 1048578 | bytes 4199013 | solution.py:84
  231.6 2.4 bitcast_dynamic-update-slice_fusion.3
  234.0 2.5 bitcast_dynamic-update-slice_fusion.3
  236.5 2.5 bitcast_dynamic-update-slice_fusion.3
  238.9 2.4 bitcast_dynamic-update-slice_fusion.3
  241.5 120.9 %while.29 = (s32[]{:T(128)}, f32[8,32,512]{2,1,0:T(8,128)S(1)}, f32[8,32,512]{2,1,0:T(8,128)S(1)}, f32[512]{0:T(512)S(1)}, f32[512]{0:T(512)S(1)}, /*index=5*/f3...) while((s32[]{:T(128)}, f32[8,32,512]{2,1,0:T(8,128)S(1)}, f32[8,32,512]{2,1,0:T(8,128)S(1)}, ...), condition=%wide.region_3.4_spmd, body=%wide.region_2.3_spmd.sunk | while | flops 1048578 | bytes 7344293 | solution.py:97
  241.8 1.9 collective-permute-start
  243.7 3.5 collective-permute-start.1
  247.2 6.0 %collective-permute-done = f32[8,32,512]{2,1,0:T(8,128)S(1)} collective-permute-done((f32[8,32,512]{2,1,0:T(8,128)S(1)}, f32[8,32,512]{2,1,0:T(8,128)S(1)}, u32[]{:S(2)}, u32[]{:S(2)}) %collective-permute-start) | collective-permute-done | bytes 524320 | tf_op jit(solution)/shard_map/while/body/eval_jaxpr/ppermute | solution.py:10
  253.2 5.6 %collective-permute-done.1 = f32[8,32,512]{2,1,0:T(8,128)S(1)} collective-permute-done((f32[8,32,512]{2,1,0:T(8,128)S(1)}, f32[8,32,512]{2,1,0:T(8,128)S(1)}, u32[]{:S(2)}, u32[]{:S(2)}) %collective-permute-start.1) | collective-permute-done | bytes 524320 | tf_op jit(solution)/shard_map/while/body/eval_jaxpr/ppermute | solution.py:10
  259.0 1.9 collective-permute-start
  261.0 2.6 collective-permute-start.1
  263.6 6.9 %collective-permute-done = f32[8,32,512]{2,1,0:T(8,128)S(1)} collective-permute-done((f32[8,32,512]{2,1,0:T(8,128)S(1)}, f32[8,32,512]{2,1,0:T(8,128)S(1)}, u32[]{:S(2)}, u32[]{:S(2)}) %collective-permute-start) | collective-permute-done | bytes 524320 | tf_op jit(solution)/shard_map/while/body/eval_jaxpr/ppermute | solution.py:10
  270.4 5.6 %collective-permute-done.1 = f32[8,32,512]{2,1,0:T(8,128)S(1)} collective-permute-done((f32[8,32,512]{2,1,0:T(8,128)S(1)}, f32[8,32,512]{2,1,0:T(8,128)S(1)}, u32[]{:S(2)}, u32[]{:S(2)}) %collective-permute-start.1) | collective-permute-done | bytes 524320 | tf_op jit(solution)/shard_map/while/body/eval_jaxpr/ppermute | solution.py:10
  276.3 1.9 collective-permute-start
  278.2 1.9 collective-permute-start.1
  280.2 7.5 %collective-permute-done = f32[8,32,512]{2,1,0:T(8,128)S(1)} collective-permute-done((f32[8,32,512]{2,1,0:T(8,128)S(1)}, f32[8,32,512]{2,1,0:T(8,128)S(1)}, u32[]{:S(2)}, u32[]{:S(2)}) %collective-permute-start) | collective-permute-done | bytes 524320 | tf_op jit(solution)/shard_map/while/body/eval_jaxpr/ppermute | solution.py:10
  287.7 5.6 %collective-permute-done.1 = f32[8,32,512]{2,1,0:T(8,128)S(1)} collective-permute-done((f32[8,32,512]{2,1,0:T(8,128)S(1)}, f32[8,32,512]{2,1,0:T(8,128)S(1)}, u32[]{:S(2)}, u32[]{:S(2)}) %collective-permute-start.1) | collective-permute-done | bytes 524320 | tf_op jit(solution)/shard_map/while/body/eval_jaxpr/ppermute | solution.py:10
  293.6 1.9 collective-permute-start
  295.5 1.9 collective-permute-start.1
  297.4 7.5 %collective-permute-done = f32[8,32,512]{2,1,0:T(8,128)S(1)} collective-permute-done((f32[8,32,512]{2,1,0:T(8,128)S(1)}, f32[8,32,512]{2,1,0:T(8,128)S(1)}, u32[]{:S(2)}, u32[]{:S(2)}) %collective-permute-start) | collective-permute-done | bytes 524320 | tf_op jit(solution)/shard_map/while/body/eval_jaxpr/ppermute | solution.py:10
  305.0 5.6 %collective-permute-done.1 = f32[8,32,512]{2,1,0:T(8,128)S(1)} collective-permute-done((f32[8,32,512]{2,1,0:T(8,128)S(1)}, f32[8,32,512]{2,1,0:T(8,128)S(1)}, u32[]{:S(2)}, u32[]{:S(2)}) %collective-permute-start.1) | collective-permute-done | bytes 524320 | tf_op jit(solution)/shard_map/while/body/eval_jaxpr/ppermute | solution.py:10
  310.9 1.9 collective-permute-start
  312.8 1.9 collective-permute-start.1
  314.7 7.5 %collective-permute-done = f32[8,32,512]{2,1,0:T(8,128)S(1)} collective-permute-done((f32[8,32,512]{2,1,0:T(8,128)S(1)}, f32[8,32,512]{2,1,0:T(8,128)S(1)}, u32[]{:S(2)}, u32[]{:S(2)}) %collective-permute-start) | collective-permute-done | bytes 524320 | tf_op jit(solution)/shard_map/while/body/eval_jaxpr/ppermute | solution.py:10
  322.3 5.6 %collective-permute-done.1 = f32[8,32,512]{2,1,0:T(8,128)S(1)} collective-permute-done((f32[8,32,512]{2,1,0:T(8,128)S(1)}, f32[8,32,512]{2,1,0:T(8,128)S(1)}, u32[]{:S(2)}, u32[]{:S(2)}) %collective-permute-start.1) | collective-permute-done | bytes 524320 | tf_op jit(solution)/shard_map/while/body/eval_jaxpr/ppermute | solution.py:10
  328.1 1.9 collective-permute-start
  330.1 1.9 collective-permute-start.1
  332.0 7.5 %collective-permute-done = f32[8,32,512]{2,1,0:T(8,128)S(1)} collective-permute-done((f32[8,32,512]{2,1,0:T(8,128)S(1)}, f32[8,32,512]{2,1,0:T(8,128)S(1)}, u32[]{:S(2)}, u32[]{:S(2)}) %collective-permute-start) | collective-permute-done | bytes 524320 | tf_op jit(solution)/shard_map/while/body/eval_jaxpr/ppermute | solution.py:10
  339.5 5.6 %collective-permute-done.1 = f32[8,32,512]{2,1,0:T(8,128)S(1)} collective-permute-done((f32[8,32,512]{2,1,0:T(8,128)S(1)}, f32[8,32,512]{2,1,0:T(8,128)S(1)}, u32[]{:S(2)}, u32[]{:S(2)}) %collective-permute-start.1) | collective-permute-done | bytes 524320 | tf_op jit(solution)/shard_map/while/body/eval_jaxpr/ppermute | solution.py:10
  345.4 1.9 collective-permute-start
  347.3 1.9 collective-permute-start.1
  349.3 7.5 %collective-permute-done = f32[8,32,512]{2,1,0:T(8,128)S(1)} collective-permute-done((f32[8,32,512]{2,1,0:T(8,128)S(1)}, f32[8,32,512]{2,1,0:T(8,128)S(1)}, u32[]{:S(2)}, u32[]{:S(2)}) %collective-permute-start) | collective-permute-done | bytes 524320 | tf_op jit(solution)/shard_map/while/body/eval_jaxpr/ppermute | solution.py:10
  356.8 5.6 %collective-permute-done.1 = f32[8,32,512]{2,1,0:T(8,128)S(1)} collective-permute-done((f32[8,32,512]{2,1,0:T(8,128)S(1)}, f32[8,32,512]{2,1,0:T(8,128)S(1)}, u32[]{:S(2)}, u32[]{:S(2)}) %collective-permute-start.1) | collective-permute-done | bytes 524320 | tf_op jit(solution)/shard_map/while/body/eval_jaxpr/ppermute | solution.py:10
  362.4 3.0 fusion.59
  365.5 4.4 %collective-permute-start.4 = (bf16[4,1,32,2,512]{4,2,3,1,0:T(8,128)(2,1)S(1)}, bf16[4,1,32,2,512]{4,2,3,1,0:T(8,128)(2,1)S(1)}, u32[]{:S(2)}, u32[]{:S(2)}) collective-permute-start(bf16[4,1,32,2,512]{4,2,3,1,0:T(8,128)(2,1)S(1)} %get-tuple-element.141), channel_id=1, source_target_pairs={{0,1},{1,2},{2,3},{4,5},{5,6},{6,7},{8,9},{9,10},{10,11},{12,13},{... | collective-permute-start | bytes 786440 | tf_op jit(solution)/shard_map/ppermute | solution.py:21
  369.9 2.4 collective-permute-start.5
  372.3 2.6 fusion.32
  374.9 3.9 fusion.5
  378.8 1.8 select_maximum_fusion
  380.7 1.3 fusion.24
  382.0 1.2 fusion.26
  383.2 1.3 fusion.28
  385.7 1.2 fusion.22
  387.0 2.6 fusion.11
  389.6 8.6 %fusion.19 = bf16[4,8,32,512]{3,2,1,0:T(8,128)(2,1)} fusion(bf16[4,8,32,512]{3,2,1,0:T(8,128)(2,1)S(1)} %copy-done.2, f32[4,8,32,512,1]{3,2,4,1,0:T(8,128)} %fusion.11, f32[4,8,32,512,1]{3,2,4,1,0:T(8,128)S(1)} %fusion.22, f32[4,8,32,512,1]{3,2,4,1,0:T(8,128)S(1)} %fusion.24, f32[4,8,32,512,1]{3,2,4,1,0:T(8,128)S(1)} %fusion.32, ...), kind=kOutput, calls=%fused_computation.33 | convolution fusion | flops 1113587712 | bytes 22022144 | tf_op jit(solution)/shard_map/dot_general | solution.py:59
  (49 shorter events, 7.9 us)
Async XLA Ops:
  6.5 8.4 %copy-start.6 = (f32[512]{0:T(512)S(1)}, f32[512]{0:T(512)}, u32[]{:S(2)}) copy-start(f32[512]{0:T(512)} %param.14) | copy-start | bytes 6148
  6.5 8.4 %copy-start.5 = (f32[512]{0:T(512)S(1)}, f32[512]{0:T(512)}, u32[]{:S(2)}) copy-start(f32[512]{0:T(512)} %param.15) | copy-start | bytes 6148
  6.5 8.4 %copy-start.4 = (f32[8,32,2,512]{3,2,1,0:T(2,128)S(1)}, f32[8,32,2,512]{3,2,1,0:T(2,128)}, u32[]{:S(2)}) copy-start(f32[8,32,2,512]{3,2,1,0:T(2,128)} %param.16) | copy-start | bytes 3145732
  6.5 167.5 %all-gather.3.cloned.1.call-start = ((), (), s32[]{:S(2)}) async-start(), calls=%async_computation | async-start | bytes 11796480 | tf_op jit(solution)/shard_map/all_gather | solution.py:114
  7.3 365.0 %all-gather.5.cloned.1.call-start = ((), (), s32[]{:S(2)}) async-start(), calls=%async_computation.1 | async-start | bytes 11796480 | tf_op jit(solution)/shard_map/all_gather | solution.py:120
  9.0 7.3 %collective-permute-start.2 = (bf16[4,1,32,512]{3,2,1,0:T(8,128)(2,1)S(1)}, bf16[4,1,32,512]{3,2,1,0:T(8,128)(2,1)S(1)}, u32[]{:S(2)}, u32[]{:S(2)}) collective-permute-start(bf16[4,1,32,512]{3,2,1,0:T(8,128)(2,1)S(1)} %get-tuple-element.145), channel_id=1, source_target_pairs={{0,1},{1,2},{2,3},{4,5},{5,6},{6,7},{8,9},{9,10},{10,11},{12,13},{... | collective-permute-start | bytes 393224 | tf_op jit(solution)/shard_map/ppermute | solution.py:21
  12.5 6.9 %collective-permute-start.3 = (bf16[4,1,32,512]{3,2,1,0:T(8,128)(2,1)S(1)}, bf16[4,1,32,512]{3,2,1,0:T(8,128)(2,1)S(1)}, u32[]{:S(2)}, u32[]{:S(2)}) collective-permute-start(bf16[4,1,32,512]{3,2,1,0:T(8,128)(2,1)S(1)} %get-tuple-element.146), channel_id=1, source_target_pairs={{1,0},{2,1},{3,2},{5,4},{6,5},{7,6},{9,8},{10,9},{11,10},{13,12},{... | collective-permute-start | bytes 393224 | tf_op jit(solution)/shard_map/ppermute | solution.py:23
  15.0 4.4 %copy-start = (bf16[4,8,32,512]{3,2,1,0:T(8,128)(2,1)S(1)}, bf16[4,8,32,512]{3,2,1,0:T(8,128)(2,1)}, u32[]{:S(2)}) copy-start(bf16[4,8,32,512]{3,2,1,0:T(8,128)(2,1)} %param.11) | copy-start | bytes 3145732
  174.1 2.9 copy-start.1
  174.1 6.1 %copy-start.3 = (bf16[2,512,4608]{2,1,0:T(8,128)(2,1)S(1)}, bf16[2,512,4608]{2,1,0:T(8,128)(2,1)}, u32[]{:S(2)}) copy-start(bf16[2,512,4608]{2,1,0:T(8,128)(2,1)} %all-gather.3.cloned.1.call-done) | copy-start | bytes 28311556
  241.8 11.4 %collective-permute-start = (f32[8,32,512]{2,1,0:T(8,128)S(1)}, f32[8,32,512]{2,1,0:T(8,128)S(1)}, u32[]{:S(2)}, u32[]{:S(2)}) collective-permute-start(f32[8,32,512]{2,1,0:T(8,128)S(1)} %get-tuple-element.268), channel_id=1, source_target_pairs={{0,4},{4,8},{8,12},{12,16},{16,20},{20,24},{24,28},{1,5},{5,9},{9,... | collective-permute-start | bytes 1572872 | tf_op jit(solution)/shard_map/while/body/eval_jaxpr/ppermute | solution.py:10
  243.7 15.1 %collective-permute-start.1 = (f32[8,32,512]{2,1,0:T(8,128)S(1)}, f32[8,32,512]{2,1,0:T(8,128)S(1)}, u32[]{:S(2)}, u32[]{:S(2)}) collective-permute-start(f32[8,32,512]{2,1,0:T(8,128)S(1)} %get-tuple-element.269), channel_id=1, source_target_pairs={{0,4},{4,8},{8,12},{12,16},{16,20},{20,24},{24,28},{1,5},{5,9},{9,... | collective-permute-start | bytes 1572872 | tf_op jit(solution)/shard_map/while/body/eval_jaxpr/ppermute | solution.py:10
  259.0 11.4 %collective-permute-start = (f32[8,32,512]{2,1,0:T(8,128)S(1)}, f32[8,32,512]{2,1,0:T(8,128)S(1)}, u32[]{:S(2)}, u32[]{:S(2)}) collective-permute-start(f32[8,32,512]{2,1,0:T(8,128)S(1)} %get-tuple-element.268), channel_id=1, source_target_pairs={{0,4},{4,8},{8,12},{12,16},{16,20},{20,24},{24,28},{1,5},{5,9},{9,... | collective-permute-start | bytes 1572872 | tf_op jit(solution)/shard_map/while/body/eval_jaxpr/ppermute | solution.py:10
  261.0 15.1 %collective-permute-start.1 = (f32[8,32,512]{2,1,0:T(8,128)S(1)}, f32[8,32,512]{2,1,0:T(8,128)S(1)}, u32[]{:S(2)}, u32[]{:S(2)}) collective-permute-start(f32[8,32,512]{2,1,0:T(8,128)S(1)} %get-tuple-element.269), channel_id=1, source_target_pairs={{0,4},{4,8},{8,12},{12,16},{16,20},{20,24},{24,28},{1,5},{5,9},{9,... | collective-permute-start | bytes 1572872 | tf_op jit(solution)/shard_map/while/body/eval_jaxpr/ppermute | solution.py:10
  276.3 11.4 %collective-permute-start = (f32[8,32,512]{2,1,0:T(8,128)S(1)}, f32[8,32,512]{2,1,0:T(8,128)S(1)}, u32[]{:S(2)}, u32[]{:S(2)}) collective-permute-start(f32[8,32,512]{2,1,0:T(8,128)S(1)} %get-tuple-element.268), channel_id=1, source_target_pairs={{0,4},{4,8},{8,12},{12,16},{16,20},{20,24},{24,28},{1,5},{5,9},{9,... | collective-permute-start | bytes 1572872 | tf_op jit(solution)/shard_map/while/body/eval_jaxpr/ppermute | solution.py:10
  278.2 15.1 %collective-permute-start.1 = (f32[8,32,512]{2,1,0:T(8,128)S(1)}, f32[8,32,512]{2,1,0:T(8,128)S(1)}, u32[]{:S(2)}, u32[]{:S(2)}) collective-permute-start(f32[8,32,512]{2,1,0:T(8,128)S(1)} %get-tuple-element.269), channel_id=1, source_target_pairs={{0,4},{4,8},{8,12},{12,16},{16,20},{20,24},{24,28},{1,5},{5,9},{9,... | collective-permute-start | bytes 1572872 | tf_op jit(solution)/shard_map/while/body/eval_jaxpr/ppermute | solution.py:10
  293.6 11.4 %collective-permute-start = (f32[8,32,512]{2,1,0:T(8,128)S(1)}, f32[8,32,512]{2,1,0:T(8,128)S(1)}, u32[]{:S(2)}, u32[]{:S(2)}) collective-permute-start(f32[8,32,512]{2,1,0:T(8,128)S(1)} %get-tuple-element.268), channel_id=1, source_target_pairs={{0,4},{4,8},{8,12},{12,16},{16,20},{20,24},{24,28},{1,5},{5,9},{9,... | collective-permute-start | bytes 1572872 | tf_op jit(solution)/shard_map/while/body/eval_jaxpr/ppermute | solution.py:10
  295.5 15.1 %collective-permute-start.1 = (f32[8,32,512]{2,1,0:T(8,128)S(1)}, f32[8,32,512]{2,1,0:T(8,128)S(1)}, u32[]{:S(2)}, u32[]{:S(2)}) collective-permute-start(f32[8,32,512]{2,1,0:T(8,128)S(1)} %get-tuple-element.269), channel_id=1, source_target_pairs={{0,4},{4,8},{8,12},{12,16},{16,20},{20,24},{24,28},{1,5},{5,9},{9,... | collective-permute-start | bytes 1572872 | tf_op jit(solution)/shard_map/while/body/eval_jaxpr/ppermute | solution.py:10
  310.9 11.4 %collective-permute-start = (f32[8,32,512]{2,1,0:T(8,128)S(1)}, f32[8,32,512]{2,1,0:T(8,128)S(1)}, u32[]{:S(2)}, u32[]{:S(2)}) collective-permute-start(f32[8,32,512]{2,1,0:T(8,128)S(1)} %get-tuple-element.268), channel_id=1, source_target_pairs={{0,4},{4,8},{8,12},{12,16},{16,20},{20,24},{24,28},{1,5},{5,9},{9,... | collective-permute-start | bytes 1572872 | tf_op jit(solution)/shard_map/while/body/eval_jaxpr/ppermute | solution.py:10
  312.8 15.1 %collective-permute-start.1 = (f32[8,32,512]{2,1,0:T(8,128)S(1)}, f32[8,32,512]{2,1,0:T(8,128)S(1)}, u32[]{:S(2)}, u32[]{:S(2)}) collective-permute-start(f32[8,32,512]{2,1,0:T(8,128)S(1)} %get-tuple-element.269), channel_id=1, source_target_pairs={{0,4},{4,8},{8,12},{12,16},{16,20},{20,24},{24,28},{1,5},{5,9},{9,... | collective-permute-start | bytes 1572872 | tf_op jit(solution)/shard_map/while/body/eval_jaxpr/ppermute | solution.py:10
  328.1 11.4 %collective-permute-start = (f32[8,32,512]{2,1,0:T(8,128)S(1)}, f32[8,32,512]{2,1,0:T(8,128)S(1)}, u32[]{:S(2)}, u32[]{:S(2)}) collective-permute-start(f32[8,32,512]{2,1,0:T(8,128)S(1)} %get-tuple-element.268), channel_id=1, source_target_pairs={{0,4},{4,8},{8,12},{12,16},{16,20},{20,24},{24,28},{1,5},{5,9},{9,... | collective-permute-start | bytes 1572872 | tf_op jit(solution)/shard_map/while/body/eval_jaxpr/ppermute | solution.py:10
  330.1 15.1 %collective-permute-start.1 = (f32[8,32,512]{2,1,0:T(8,128)S(1)}, f32[8,32,512]{2,1,0:T(8,128)S(1)}, u32[]{:S(2)}, u32[]{:S(2)}) collective-permute-start(f32[8,32,512]{2,1,0:T(8,128)S(1)} %get-tuple-element.269), channel_id=1, source_target_pairs={{0,4},{4,8},{8,12},{12,16},{16,20},{20,24},{24,28},{1,5},{5,9},{9,... | collective-permute-start | bytes 1572872 | tf_op jit(solution)/shard_map/while/body/eval_jaxpr/ppermute | solution.py:10
  345.4 11.4 %collective-permute-start = (f32[8,32,512]{2,1,0:T(8,128)S(1)}, f32[8,32,512]{2,1,0:T(8,128)S(1)}, u32[]{:S(2)}, u32[]{:S(2)}) collective-permute-start(f32[8,32,512]{2,1,0:T(8,128)S(1)} %get-tuple-element.268), channel_id=1, source_target_pairs={{0,4},{4,8},{8,12},{12,16},{16,20},{20,24},{24,28},{1,5},{5,9},{9,... | collective-permute-start | bytes 1572872 | tf_op jit(solution)/shard_map/while/body/eval_jaxpr/ppermute | solution.py:10
  347.3 15.1 %collective-permute-start.1 = (f32[8,32,512]{2,1,0:T(8,128)S(1)}, f32[8,32,512]{2,1,0:T(8,128)S(1)}, u32[]{:S(2)}, u32[]{:S(2)}) collective-permute-start(f32[8,32,512]{2,1,0:T(8,128)S(1)} %get-tuple-element.269), channel_id=1, source_target_pairs={{0,4},{4,8},{8,12},{12,16},{16,20},{20,24},{24,28},{1,5},{5,9},{9,... | collective-permute-start | bytes 1572872 | tf_op jit(solution)/shard_map/while/body/eval_jaxpr/ppermute | solution.py:10
  365.5 9.4 %collective-permute-start.4 = (bf16[4,1,32,2,512]{4,2,3,1,0:T(8,128)(2,1)S(1)}, bf16[4,1,32,2,512]{4,2,3,1,0:T(8,128)(2,1)S(1)}, u32[]{:S(2)}, u32[]{:S(2)}) collective-permute-start(bf16[4,1,32,2,512]{4,2,3,1,0:T(8,128)(2,1)S(1)} %get-tuple-element.141), channel_id=1, source_target_pairs={{0,1},{1,2},{2,3},{4,5},{5,6},{6,7},{8,9},{9,10},{10,11},{12,13},{... | collective-permute-start | bytes 786440 | tf_op jit(solution)/shard_map/ppermute | solution.py:21
  369.9 9.0 %collective-permute-start.5 = (bf16[4,1,32,2,512]{4,2,3,1,0:T(8,128)(2,1)S(1)}, bf16[4,1,32,2,512]{4,2,3,1,0:T(8,128)(2,1)S(1)}, u32[]{:S(2)}, u32[]{:S(2)}) collective-permute-start(bf16[4,1,32,2,512]{4,2,3,1,0:T(8,128)(2,1)S(1)} %get-tuple-element.142), channel_id=1, source_target_pairs={{1,0},{2,1},{3,2},{5,4},{6,5},{7,6},{9,8},{10,9},{11,10},{13,12},{... | collective-permute-start | bytes 786440 | tf_op jit(solution)/shard_map/ppermute | solution.py:23
  372.3 8.4 %slice-start = ((s8[9437184]{0:T(1024)(128)(4,1)}), s8[4194304]{0:T(1024)(128)(4,1)S(1)}, s32[]{:S(2)}) async-start(s8[9437184]{0:T(1024)(128)(4,1)} %bitcast.210), calls=%async_computation.2 | async-start | bytes 8388608
  372.3 8.4 %slice-start.1 = ((s8[9437184]{0:T(1024)(128)(4,1)}), s8[4194304]{0:T(1024)(128)(4,1)S(1)}, s32[]{:S(2)}) async-start(s8[9437184]{0:T(1024)(128)(4,1)} %bitcast.210), calls=%async_computation.3 | async-start | bytes 8388608
  374.9 5.8 %slice-start.2 = ((s8[9437184]{0:T(1024)(128)(4,1)}), s8[1048576]{0:T(1024)(128)(4,1)S(1)}, s32[]{:S(2)}) async-start(s8[9437184]{0:T(1024)(128)(4,1)} %bitcast.210), calls=%async_computation.4 | async-start | bytes 2097152
  387.0 2.6 copy-start.2
  387.0 2.6 copy-start.7
Sparse Core Ops, SparseCore 0:
  8.9 165.1 all-gather.2
  175.6 164.9 all-gather.4
where the time goes:
time: 406 us; the launch traced here: 405 us
  waiting for transfers between devices  248 us (61%)
  matrix products  61.8 us (15%)
  starting transfers between devices  41.7 us (10%)
  local copies, waits for them, and re-layouts  21.8 us (5%)
  other arithmetic  17.6 us (4%)
  between operations  13.7 us (3%)
    all_gather x1, waiting for transfers between devices, on_device(): lax.all_gather(weight_in, 'rows', axis=1, tiled=True)  154 us
    ppermute x14, waiting for transfers between devices, passed_along(): lax.ppermute(value, axis, [(source, source + steps) for source in range(f...  89.9 us
    dot_general x9, matrix products, in_term(): lax.dot_general(window, weight_tap, (((3,), (1,)), ((), ())), preferred_e...  37.8 us
    ppermute x14, starting transfers between devices, passed_along(): lax.ppermute(value, axis, [(source, source + steps) for source in range(f...  29.1 us
    dot_general x9, matrix products, out_term(): lax.dot_general(window, piece[tap_index], (((3, 4), (0, 1)), ((), ())), p...  24 us
    dynamic_update_slice x4, other arithmetic, run_states(): lax.scan(advance, (begin_re, begin_im), (driven[..., 0, :], driven[..., 1...  9.82 us
  transfers between devices with their start and end apart: 20, of which 16 were waited for; matrix products, arithmetic and copies ran while one was open for 20% of the time, Pallas kernels for 0%

commit v1 on v0

--- a/solution.py
+++ b/solution.py
@@ -111,7 +111,10 @@
     extended = extended_2(frames_in, (("rows", 1),), 1)
     padded = pad_field(extended, 0)
     driven = in_term(
-        padded, lax.all_gather(weight_in, "rows", axis=1, tiled=True), band_rows, columns
+        padded,
+        jnp.concatenate(lax.all_gather(weight_in, axis_name="rows"), axis=1),
+        band_rows,
+        columns,
     )
     held = run_states(driven, start_state[:, :, 0, :], start_state[:, :, 1, :], log_decay, rotation)
     held = extended_2(held, (("rows", 1),), 1)

time: 406 us -> 421 us (1.037)
  local copies, waits for them, and re-layouts: 21.8 us -> 29.7 us
  matrix products: 61.8 us -> 68.6 us
    all_gather x0 -> x1, local copies, waits for them, and re-layouts: none -> 7.95 us  [on_device(): lax.all_gather(weight_in, axis_name='rows')]
    dot_general x9, matrix products: 37.8 us -> 44.6 us  [in_term(): lax.dot_general(window, weight_tap, (((3,), (1,)), ((), ())), preferred_e...]
  transfers between devices with their start and end apart: 20 -> 20, of which waited for: 16 -> 16; matrix products, arithmetic and copies ran while one was open for 20% -> 23% of each run, Pallas kernels for 0% -> 0%
where the time goes in v1:
time: 421 us; the launch traced here: 420 us
  waiting for transfers between devices  248 us (59%)
  matrix products  68.6 us (16%)
  starting transfers between devices  41.6 us (10%)
  local copies, waits for them, and re-layouts  29.7 us (7%)
  other arithmetic  17.6 us (4%)
  between operations  13.7 us (3%)
    all_gather x1, waiting for transfers between devices, on_device(): lax.all_gather(weight_in, axis_name='rows')  154 us
    ppermute x14, waiting for transfers between devices, passed_along(): lax.ppermute(value, axis, [(source, source + steps) for source in range(f...  89.9 us
    dot_general x9, matrix products, in_term(): lax.dot_general(window, weight_tap, (((3,), (1,)), ((), ())), preferred_e...  44.6 us
    ppermute x14, starting transfers between devices, passed_along(): lax.ppermute(value, axis, [(source, source + steps) for source in range(f...  29.1 us
    dot_general x9, matrix products, out_term(): lax.dot_general(window, piece[tap_index], (((3, 4), (0, 1)), ((), ())), p...  24 us
    dynamic_update_slice x4, other arithmetic, run_states(): lax.scan(advance, (begin_re, begin_im), (driven[..., 0, :], driven[..., 1...  9.82 us
  transfers between devices with their start and end apart: 20, of which 16 were waited for; matrix products, arithmetic and copies ran while one was open for 23% of the time, Pallas kernels for 0%

profile of v1, /device:TPU:12, one launch (start us, length us, event | category | flops | bytes accessed | tf_op | source)
XLA Modules:
  0.0 419.7 jit_solution(14305211949276130117)
XLA Ops:
  9.0 3.5 collective-permute-start.2
  12.5 2.4 collective-permute-start.3
  16.3 3.0 collective-permute-done.3
  20.2 153.8 %all-gather.6.cloned.1.call-done = bf16[8,128,4608]{2,1,0:T(8,128)(2,1)} async-done(((bf16[2,128,4608]{2,1,0:T(8,128)(2,1)}), bf16[8,128,4608]{2,1,0:T(8,128)(2,1)}) %all-gather.6.cloned.1.call-update) | async-done | bytes 9437200 | tf_op jit(solution)/shard_map/all_gather | solution.py:115
  174.1 7.9 %copy.16 = bf16[4,2,128,4608]{3,2,0,1:T(8,128)(2,1)} copy(bf16[4,2,128,4608]{3,2,1,0:T(8,128)(2,1)} %bitcast.213) | data formatting | bytes 18874368 | tf_op jit(solution)/shard_map/all_gather | solution.py:115
  182.0 5.4 %fusion.51 = f32[4,8,32,1024]{3,2,1,0:T(8,128)} fusion(bf16[4,8,32,512]{3,2,1,0:T(8,128)(2,1)} %param.11, bf16[4,1,32,512]{3,2,1,0:T(8,128)(2,1)S(1)} %collective-permute-done.2, bf16[1024,4608]{1,0:T(8,128)(2,1)} %bitcast.204), kind=kOutput, calls=%fused_computation.83 | convolution fusion | flops 1076101120 | bytes 6422528 | tf_op jit(solution)/shard_map/dot_general | solution.py:47
  187.4 5.5 %fusion.55 = f32[4,8,32,1024]{3,2,1,0:T(8,128)} fusion(bf16[4,1,32,512]{3,2,1,0:T(8,128)(2,1)S(1)} %collective-permute-done.3, bf16[4,8,32,512]{3,2,1,0:T(8,128)(2,1)} %param.11, bf16[1024,4608]{1,0:T(8,128)(2,1)} %bitcast.205), kind=kOutput, calls=%fused_computation.87 | convolution fusion | flops 1076101120 | bytes 6422528 | tf_op jit(solution)/shard_map/dot_general | solution.py:47
  192.9 3.2 fusion.63
  196.1 3.3 fusion.65
  199.4 3.4 fusion.68
  202.7 3.2 fusion.70
  206.0 3.2 fusion.72
  209.2 3.3 fusion.67
  212.5 14.1 %add_add_fusion.1 = f32[4,8,32,1024]{3,2,1,0:T(8,128)} fusion(f32[4,8,32,1024]{3,2,1,0:T(8,128)} %fusion.55, f32[4,8,32,1024]{3,2,1,0:T(8,128)} %fusion.63, f32[4,8,32,1024]{3,2,1,0:T(8,128)} %fusion.65, f32[4,8,32,1024]{3,2,1,0:T(8,128)} %fusion.67, f32[4,8,32,1024]{3,2,1,0:T(8,128)} %fusion.68, f32[4,8,32,1024]{3,2,1,0:T(8,128)} %fusion.70, ...), kind=kOutput, calls=%fused_computation.11 | convolution fusion | flops 1082130432 | bytes 39845888 | tf_op jit(solution)/shard_map/dot_general | solution.py:47
  226.6 6.6 %reshape.132 = f32[4,8,32,2,512]{4,3,2,1,0:T(2,128)} reshape(f32[4,8,32,1024]{3,2,1,0:T(8,128)} %add_add_fusion.1) | data formatting | bytes 8388608 | tf_op jit(solution)/shard_map/reshape | solution.py:50
  233.2 7.9 %fusion.83 = (f32[4,8,32,1,512]{4,3,2,1,0:T(1,128)S(1)}, f32[4,8,32,1,512]{4,3,2,1,0:T(1,128)S(1)}) fusion(f32[4,8,32,2,512]{4,3,2,1,0:T(2,128)} %reshape.132), kind=kLoop, calls=%fused_computation.146 | loop fusion | bytes 8388608 | tf_op jit(solution)/shard_map/slice | solution.py:85
  241.1 2.0 copy_bitcast_fusion
  243.0 1.7 broadcast.93
  244.7 1.6 broadcast.93.clone
  246.3 9.8 %while.28 = (s32[]{:T(128)}, f32[8,32,512]{2,1,0:T(8,128)S(1)}, f32[8,32,512]{2,1,0:T(8,128)S(1)}, f32[4,8,32,512]{3,2,1,0:T(8,128)}, f32[4,8,32,512]{3,2,1,0:T(...) while((s32[]{:T(128)}, f32[8,32,512]{2,1,0:T(8,128)S(1)}, ...), condition=%wide.region_1.2_spmd, body=%wide.region_0.1_spmd.sunk | while | flops 1048578 | bytes 4199013 | solution.py:84
  246.3 2.4 bitcast_dynamic-update-slice_fusion.3
  248.7 2.5 bitcast_dynamic-update-slice_fusion.3
  251.2 2.5 bitcast_dynamic-update-slice_fusion.3
  253.7 2.4 bitcast_dynamic-update-slice_fusion.3
  256.2 120.9 %while.29 = (s32[]{:T(128)}, f32[8,32,512]{2,1,0:T(8,128)S(1)}, f32[8,32,512]{2,1,0:T(8,128)S(1)}, f32[512]{0:T(512)S(1)}, f32[512]{0:T(512)S(1)}, /*index=5*/f3...) while((s32[]{:T(128)}, f32[8,32,512]{2,1,0:T(8,128)S(1)}, f32[8,32,512]{2,1,0:T(8,128)S(1)}, ...), condition=%wide.region_3.4_spmd, body=%wide.region_2.3_spmd.sunk | while | flops 1048578 | bytes 7344293 | solution.py:97
  256.5 1.9 collective-permute-start
  258.4 3.5 collective-permute-start.1
  261.9 6.0 %collective-permute-done = f32[8,32,512]{2,1,0:T(8,128)S(1)} collective-permute-done((f32[8,32,512]{2,1,0:T(8,128)S(1)}, f32[8,32,512]{2,1,0:T(8,128)S(1)}, u32[]{:S(2)}, u32[]{:S(2)}) %collective-permute-start) | collective-permute-done | bytes 524320 | tf_op jit(solution)/shard_map/while/body/eval_jaxpr/ppermute | solution.py:10
  267.9 5.6 %collective-permute-done.1 = f32[8,32,512]{2,1,0:T(8,128)S(1)} collective-permute-done((f32[8,32,512]{2,1,0:T(8,128)S(1)}, f32[8,32,512]{2,1,0:T(8,128)S(1)}, u32[]{:S(2)}, u32[]{:S(2)}) %collective-permute-start.1) | collective-permute-done | bytes 524320 | tf_op jit(solution)/shard_map/while/body/eval_jaxpr/ppermute | solution.py:10
  273.8 1.9 collective-permute-start
  275.7 2.6 collective-permute-start.1
  278.3 6.9 %collective-permute-done = f32[8,32,512]{2,1,0:T(8,128)S(1)} collective-permute-done((f32[8,32,512]{2,1,0:T(8,128)S(1)}, f32[8,32,512]{2,1,0:T(8,128)S(1)}, u32[]{:S(2)}, u32[]{:S(2)}) %collective-permute-start) | collective-permute-done | bytes 524320 | tf_op jit(solution)/shard_map/while/body/eval_jaxpr/ppermute | solution.py:10
  285.2 5.6 %collective-permute-done.1 = f32[8,32,512]{2,1,0:T(8,128)S(1)} collective-permute-done((f32[8,32,512]{2,1,0:T(8,128)S(1)}, f32[8,32,512]{2,1,0:T(8,128)S(1)}, u32[]{:S(2)}, u32[]{:S(2)}) %collective-permute-start.1) | collective-permute-done | bytes 524320 | tf_op jit(solution)/shard_map/while/body/eval_jaxpr/ppermute | solution.py:10
  291.0 1.9 collective-permute-start
  293.0 1.9 collective-permute-start.1
  294.9 7.5 %collective-permute-done = f32[8,32,512]{2,1,0:T(8,128)S(1)} collective-permute-done((f32[8,32,512]{2,1,0:T(8,128)S(1)}, f32[8,32,512]{2,1,0:T(8,128)S(1)}, u32[]{:S(2)}, u32[]{:S(2)}) %collective-permute-start) | collective-permute-done | bytes 524320 | tf_op jit(solution)/shard_map/while/body/eval_jaxpr/ppermute | solution.py:10
  302.4 5.6 %collective-permute-done.1 = f32[8,32,512]{2,1,0:T(8,128)S(1)} collective-permute-done((f32[8,32,512]{2,1,0:T(8,128)S(1)}, f32[8,32,512]{2,1,0:T(8,128)S(1)}, u32[]{:S(2)}, u32[]{:S(2)}) %collective-permute-start.1) | collective-permute-done | bytes 524320 | tf_op jit(solution)/shard_map/while/body/eval_jaxpr/ppermute | solution.py:10
  308.3 1.9 collective-permute-start
  310.2 1.9 collective-permute-start.1
  312.2 7.5 %collective-permute-done = f32[8,32,512]{2,1,0:T(8,128)S(1)} collective-permute-done((f32[8,32,512]{2,1,0:T(8,128)S(1)}, f32[8,32,512]{2,1,0:T(8,128)S(1)}, u32[]{:S(2)}, u32[]{:S(2)}) %collective-permute-start) | collective-permute-done | bytes 524320 | tf_op jit(solution)/shard_map/while/body/eval_jaxpr/ppermute | solution.py:10
  319.7 5.6 %collective-permute-done.1 = f32[8,32,512]{2,1,0:T(8,128)S(1)} collective-permute-done((f32[8,32,512]{2,1,0:T(8,128)S(1)}, f32[8,32,512]{2,1,0:T(8,128)S(1)}, u32[]{:S(2)}, u32[]{:S(2)}) %collective-permute-start.1) | collective-permute-done | bytes 524320 | tf_op jit(solution)/shard_map/while/body/eval_jaxpr/ppermute | solution.py:10
  325.6 1.9 collective-permute-start
  327.5 1.9 collective-permute-start.1
  329.4 7.5 %collective-permute-done = f32[8,32,512]{2,1,0:T(8,128)S(1)} collective-permute-done((f32[8,32,512]{2,1,0:T(8,128)S(1)}, f32[8,32,512]{2,1,0:T(8,128)S(1)}, u32[]{:S(2)}, u32[]{:S(2)}) %collective-permute-start) | collective-permute-done | bytes 524320 | tf_op jit(solution)/shard_map/while/body/eval_jaxpr/ppermute | solution.py:10
  337.0 5.6 %collective-permute-done.1 = f32[8,32,512]{2,1,0:T(8,128)S(1)} collective-permute-done((f32[8,32,512]{2,1,0:T(8,128)S(1)}, f32[8,32,512]{2,1,0:T(8,128)S(1)}, u32[]{:S(2)}, u32[]{:S(2)}) %collective-permute-start.1) | collective-permute-done | bytes 524320 | tf_op jit(solution)/shard_map/while/body/eval_jaxpr/ppermute | solution.py:10
  342.9 1.9 collective-permute-start
  344.8 1.9 collective-permute-start.1
  346.7 7.5 %collective-permute-done = f32[8,32,512]{2,1,0:T(8,128)S(1)} collective-permute-done((f32[8,32,512]{2,1,0:T(8,128)S(1)}, f32[8,32,512]{2,1,0:T(8,128)S(1)}, u32[]{:S(2)}, u32[]{:S(2)}) %collective-permute-start) | collective-permute-done | bytes 524320 | tf_op jit(solution)/shard_map/while/body/eval_jaxpr/ppermute | solution.py:10
  354.3 5.6 %collective-permute-done.1 = f32[8,32,512]{2,1,0:T(8,128)S(1)} collective-permute-done((f32[8,32,512]{2,1,0:T(8,128)S(1)}, f32[8,32,512]{2,1,0:T(8,128)S(1)}, u32[]{:S(2)}, u32[]{:S(2)}) %collective-permute-start.1) | collective-permute-done | bytes 524320 | tf_op jit(solution)/shard_map/while/body/eval_jaxpr/ppermute | solution.py:10
  360.1 1.9 collective-permute-start
  362.1 1.9 collective-permute-start.1
  364.0 7.5 %collective-permute-done = f32[8,32,512]{2,1,0:T(8,128)S(1)} collective-permute-done((f32[8,32,512]{2,1,0:T(8,128)S(1)}, f32[8,32,512]{2,1,0:T(8,128)S(1)}, u32[]{:S(2)}, u32[]{:S(2)}) %collective-permute-start) | collective-permute-done | bytes 524320 | tf_op jit(solution)/shard_map/while/body/eval_jaxpr/ppermute | solution.py:10
  371.5 5.6 %collective-permute-done.1 = f32[8,32,512]{2,1,0:T(8,128)S(1)} collective-permute-done((f32[8,32,512]{2,1,0:T(8,128)S(1)}, f32[8,32,512]{2,1,0:T(8,128)S(1)}, u32[]{:S(2)}, u32[]{:S(2)}) %collective-permute-start.1) | collective-permute-done | bytes 524320 | tf_op jit(solution)/shard_map/while/body/eval_jaxpr/ppermute | solution.py:10
  377.1 3.0 fusion.59
  380.2 4.6 %collective-permute-start.4 = (bf16[4,1,32,2,512]{4,2,3,1,0:T(8,128)(2,1)S(1)}, bf16[4,1,32,2,512]{4,2,3,1,0:T(8,128)(2,1)S(1)}, u32[]{:S(2)}, u32[]{:S(2)}) collective-permute-start(bf16[4,1,32,2,512]{4,2,3,1,0:T(8,128)(2,1)S(1)} %get-tuple-element.141), channel_id=1, source_target_pairs={{0,1},{1,2},{2,3},{4,5},{5,6},{6,7},{8,9},{9,10},{10,11},{12,13},{... | collective-permute-start | bytes 786440 | tf_op jit(solution)/shard_map/ppermute | solution.py:21
  384.8 2.0 collective-permute-start.5
  386.9 2.6 fusion.32
  389.6 3.9 fusion.5
  393.5 1.8 select_maximum_fusion
  395.4 1.3 fusion.24
  397.9 1.3 fusion.28
  400.4 1.2 fusion.22
  401.7 2.6 fusion.11
  404.3 8.6 %fusion.19 = bf16[4,8,32,512]{3,2,1,0:T(8,128)(2,1)} fusion(bf16[4,8,32,512]{3,2,1,0:T(8,128)(2,1)S(1)} %copy-done.3, f32[4,8,32,512,1]{3,2,4,1,0:T(8,128)} %fusion.11, f32[4,8,32,512,1]{3,2,4,1,0:T(8,128)S(1)} %fusion.22, f32[4,8,32,512,1]{3,2,4,1,0:T(8,128)S(1)} %fusion.24, f32[4,8,32,512,1]{3,2,4,1,0:T(8,128)S(1)} %fusion.32, ...), kind=kOutput, calls=%fused_computation.33 | convolution fusion | flops 1113587712 | bytes 22022144 | tf_op jit(solution)/shard_map/dot_general | solution.py:59
  (50 shorter events, 9.1 us)
Async XLA Ops:
  6.5 8.4 %copy-start.6 = (f32[512]{0:T(512)S(1)}, f32[512]{0:T(512)}, u32[]{:S(2)}) copy-start(f32[512]{0:T(512)} %param.14) | copy-start | bytes 6148
  6.5 8.4 %copy-start.5 = (f32[512]{0:T(512)S(1)}, f32[512]{0:T(512)}, u32[]{:S(2)}) copy-start(f32[512]{0:T(512)} %param.15) | copy-start | bytes 6148
  6.5 8.4 %copy-start.4 = (f32[8,32,2,512]{3,2,1,0:T(2,128)S(1)}, f32[8,32,2,512]{3,2,1,0:T(2,128)}, u32[]{:S(2)}) copy-start(f32[8,32,2,512]{3,2,1,0:T(2,128)} %param.16) | copy-start | bytes 3145732
  6.5 167.5 %all-gather.6.cloned.1.call-start = ((), (), s32[]{:S(2)}) async-start(), calls=%async_computation.1 | async-start | bytes 11796480 | tf_op jit(solution)/shard_map/all_gather | solution.py:115
  7.3 379.7 %all-gather.4.cloned.1.call-start = ((), (), s32[]{:S(2)}) async-start(), calls=%async_computation | async-start | bytes 11796480 | tf_op jit(solution)/shard_map/all_gather | solution.py:123
  9.0 7.3 %collective-permute-start.2 = (bf16[4,1,32,512]{3,2,1,0:T(8,128)(2,1)S(1)}, bf16[4,1,32,512]{3,2,1,0:T(8,128)(2,1)S(1)}, u32[]{:S(2)}, u32[]{:S(2)}) collective-permute-start(bf16[4,1,32,512]{3,2,1,0:T(8,128)(2,1)S(1)} %get-tuple-element.145), channel_id=1, source_target_pairs={{0,1},{1,2},{2,3},{4,5},{5,6},{6,7},{8,9},{9,10},{10,11},{12,13},{... | collective-permute-start | bytes 393224 | tf_op jit(solution)/shard_map/ppermute | solution.py:21
  12.5 6.9 %collective-permute-start.3 = (bf16[4,1,32,512]{3,2,1,0:T(8,128)(2,1)S(1)}, bf16[4,1,32,512]{3,2,1,0:T(8,128)(2,1)S(1)}, u32[]{:S(2)}, u32[]{:S(2)}) collective-permute-start(bf16[4,1,32,512]{3,2,1,0:T(8,128)(2,1)S(1)} %get-tuple-element.146), channel_id=1, source_target_pairs={{1,0},{2,1},{3,2},{5,4},{6,5},{7,6},{9,8},{10,9},{11,10},{13,12},{... | collective-permute-start | bytes 393224 | tf_op jit(solution)/shard_map/ppermute | solution.py:23
  15.0 4.4 %copy-start.1 = (bf16[4,8,32,512]{3,2,1,0:T(8,128)(2,1)S(1)}, bf16[4,8,32,512]{3,2,1,0:T(8,128)(2,1)}, u32[]{:S(2)}) copy-start(bf16[4,8,32,512]{3,2,1,0:T(8,128)(2,1)} %param.11) | copy-start | bytes 3145732
  182.0 10.9 %copy-start = (bf16[4,2,128,4608]{3,2,0,1:T(8,128)(2,1)S(1)}, bf16[4,2,128,4608]{3,2,0,1:T(8,128)(2,1)}, u32[]{:S(2)}) copy-start(bf16[4,2,128,4608]{3,2,0,1:T(8,128)(2,1)} %copy.16) | copy-start | bytes 28311556
  206.0 3.2 copy-start.2
  256.5 11.4 %collective-permute-start = (f32[8,32,512]{2,1,0:T(8,128)S(1)}, f32[8,32,512]{2,1,0:T(8,128)S(1)}, u32[]{:S(2)}, u32[]{:S(2)}) collective-permute-start(f32[8,32,512]{2,1,0:T(8,128)S(1)} %get-tuple-element.268), channel_id=1, source_target_pairs={{0,4},{4,8},{8,12},{12,16},{16,20},{20,24},{24,28},{1,5},{5,9},{9,... | collective-permute-start | bytes 1572872 | tf_op jit(solution)/shard_map/while/body/eval_jaxpr/ppermute | solution.py:10
  258.4 15.1 %collective-permute-start.1 = (f32[8,32,512]{2,1,0:T(8,128)S(1)}, f32[8,32,512]{2,1,0:T(8,128)S(1)}, u32[]{:S(2)}, u32[]{:S(2)}) collective-permute-start(f32[8,32,512]{2,1,0:T(8,128)S(1)} %get-tuple-element.269), channel_id=1, source_target_pairs={{0,4},{4,8},{8,12},{12,16},{16,20},{20,24},{24,28},{1,5},{5,9},{9,... | collective-permute-start | bytes 1572872 | tf_op jit(solution)/shard_map/while/body/eval_jaxpr/ppermute | solution.py:10
  273.8 11.4 %collective-permute-start = (f32[8,32,512]{2,1,0:T(8,128)S(1)}, f32[8,32,512]{2,1,0:T(8,128)S(1)}, u32[]{:S(2)}, u32[]{:S(2)}) collective-permute-start(f32[8,32,512]{2,1,0:T(8,128)S(1)} %get-tuple-element.268), channel_id=1, source_target_pairs={{0,4},{4,8},{8,12},{12,16},{16,20},{20,24},{24,28},{1,5},{5,9},{9,... | collective-permute-start | bytes 1572872 | tf_op jit(solution)/shard_map/while/body/eval_jaxpr/ppermute | solution.py:10
  275.7 15.1 %collective-permute-start.1 = (f32[8,32,512]{2,1,0:T(8,128)S(1)}, f32[8,32,512]{2,1,0:T(8,128)S(1)}, u32[]{:S(2)}, u32[]{:S(2)}) collective-permute-start(f32[8,32,512]{2,1,0:T(8,128)S(1)} %get-tuple-element.269), channel_id=1, source_target_pairs={{0,4},{4,8},{8,12},{12,16},{16,20},{20,24},{24,28},{1,5},{5,9},{9,... | collective-permute-start | bytes 1572872 | tf_op jit(solution)/shard_map/while/body/eval_jaxpr/ppermute | solution.py:10
  291.0 11.4 %collective-permute-start = (f32[8,32,512]{2,1,0:T(8,128)S(1)}, f32[8,32,512]{2,1,0:T(8,128)S(1)}, u32[]{:S(2)}, u32[]{:S(2)}) collective-permute-start(f32[8,32,512]{2,1,0:T(8,128)S(1)} %get-tuple-element.268), channel_id=1, source_target_pairs={{0,4},{4,8},{8,12},{12,16},{16,20},{20,24},{24,28},{1,5},{5,9},{9,... | collective-permute-start | bytes 1572872 | tf_op jit(solution)/shard_map/while/body/eval_jaxpr/ppermute | solution.py:10
  293.0 15.1 %collective-permute-start.1 = (f32[8,32,512]{2,1,0:T(8,128)S(1)}, f32[8,32,512]{2,1,0:T(8,128)S(1)}, u32[]{:S(2)}, u32[]{:S(2)}) collective-permute-start(f32[8,32,512]{2,1,0:T(8,128)S(1)} %get-tuple-element.269), channel_id=1, source_target_pairs={{0,4},{4,8},{8,12},{12,16},{16,20},{20,24},{24,28},{1,5},{5,9},{9,... | collective-permute-start | bytes 1572872 | tf_op jit(solution)/shard_map/while/body/eval_jaxpr/ppermute | solution.py:10
  308.3 11.4 %collective-permute-start = (f32[8,32,512]{2,1,0:T(8,128)S(1)}, f32[8,32,512]{2,1,0:T(8,128)S(1)}, u32[]{:S(2)}, u32[]{:S(2)}) collective-permute-start(f32[8,32,512]{2,1,0:T(8,128)S(1)} %get-tuple-element.268), channel_id=1, source_target_pairs={{0,4},{4,8},{8,12},{12,16},{16,20},{20,24},{24,28},{1,5},{5,9},{9,... | collective-permute-start | bytes 1572872 | tf_op jit(solution)/shard_map/while/body/eval_jaxpr/ppermute | solution.py:10
  310.2 15.1 %collective-permute-start.1 = (f32[8,32,512]{2,1,0:T(8,128)S(1)}, f32[8,32,512]{2,1,0:T(8,128)S(1)}, u32[]{:S(2)}, u32[]{:S(2)}) collective-permute-start(f32[8,32,512]{2,1,0:T(8,128)S(1)} %get-tuple-element.269), channel_id=1, source_target_pairs={{0,4},{4,8},{8,12},{12,16},{16,20},{20,24},{24,28},{1,5},{5,9},{9,... | collective-permute-start | bytes 1572872 | tf_op jit(solution)/shard_map/while/body/eval_jaxpr/ppermute | solution.py:10
  325.6 11.4 %collective-permute-start = (f32[8,32,512]{2,1,0:T(8,128)S(1)}, f32[8,32,512]{2,1,0:T(8,128)S(1)}, u32[]{:S(2)}, u32[]{:S(2)}) collective-permute-start(f32[8,32,512]{2,1,0:T(8,128)S(1)} %get-tuple-element.268), channel_id=1, source_target_pairs={{0,4},{4,8},{8,12},{12,16},{16,20},{20,24},{24,28},{1,5},{5,9},{9,... | collective-permute-start | bytes 1572872 | tf_op jit(solution)/shard_map/while/body/eval_jaxpr/ppermute | solution.py:10
  327.5 15.1 %collective-permute-start.1 = (f32[8,32,512]{2,1,0:T(8,128)S(1)}, f32[8,32,512]{2,1,0:T(8,128)S(1)}, u32[]{:S(2)}, u32[]{:S(2)}) collective-permute-start(f32[8,32,512]{2,1,0:T(8,128)S(1)} %get-tuple-element.269), channel_id=1, source_target_pairs={{0,4},{4,8},{8,12},{12,16},{16,20},{20,24},{24,28},{1,5},{5,9},{9,... | collective-permute-start | bytes 1572872 | tf_op jit(solution)/shard_map/while/body/eval_jaxpr/ppermute | solution.py:10
  342.9 11.4 %collective-permute-start = (f32[8,32,512]{2,1,0:T(8,128)S(1)}, f32[8,32,512]{2,1,0:T(8,128)S(1)}, u32[]{:S(2)}, u32[]{:S(2)}) collective-permute-start(f32[8,32,512]{2,1,0:T(8,128)S(1)} %get-tuple-element.268), channel_id=1, source_target_pairs={{0,4},{4,8},{8,12},{12,16},{16,20},{20,24},{24,28},{1,5},{5,9},{9,... | collective-permute-start | bytes 1572872 | tf_op jit(solution)/shard_map/while/body/eval_jaxpr/ppermute | solution.py:10
  344.8 15.1 %collective-permute-start.1 = (f32[8,32,512]{2,1,0:T(8,128)S(1)}, f32[8,32,512]{2,1,0:T(8,128)S(1)}, u32[]{:S(2)}, u32[]{:S(2)}) collective-permute-start(f32[8,32,512]{2,1,0:T(8,128)S(1)} %get-tuple-element.269), channel_id=1, source_target_pairs={{0,4},{4,8},{8,12},{12,16},{16,20},{20,24},{24,28},{1,5},{5,9},{9,... | collective-permute-start | bytes 1572872 | tf_op jit(solution)/shard_map/while/body/eval_jaxpr/ppermute | solution.py:10
  360.1 11.4 %collective-permute-start = (f32[8,32,512]{2,1,0:T(8,128)S(1)}, f32[8,32,512]{2,1,0:T(8,128)S(1)}, u32[]{:S(2)}, u32[]{:S(2)}) collective-permute-start(f32[8,32,512]{2,1,0:T(8,128)S(1)} %get-tuple-element.268), channel_id=1, source_target_pairs={{0,4},{4,8},{8,12},{12,16},{16,20},{20,24},{24,28},{1,5},{5,9},{9,... | collective-permute-start | bytes 1572872 | tf_op jit(solution)/shard_map/while/body/eval_jaxpr/ppermute | solution.py:10
  362.1 15.1 %collective-permute-start.1 = (f32[8,32,512]{2,1,0:T(8,128)S(1)}, f32[8,32,512]{2,1,0:T(8,128)S(1)}, u32[]{:S(2)}, u32[]{:S(2)}) collective-permute-start(f32[8,32,512]{2,1,0:T(8,128)S(1)} %get-tuple-element.269), channel_id=1, source_target_pairs={{0,4},{4,8},{8,12},{12,16},{16,20},{20,24},{24,28},{1,5},{5,9},{9,... | collective-permute-start | bytes 1572872 | tf_op jit(solution)/shard_map/while/body/eval_jaxpr/ppermute | solution.py:10
  380.2 9.4 %collective-permute-start.4 = (bf16[4,1,32,2,512]{4,2,3,1,0:T(8,128)(2,1)S(1)}, bf16[4,1,32,2,512]{4,2,3,1,0:T(8,128)(2,1)S(1)}, u32[]{:S(2)}, u32[]{:S(2)}) collective-permute-start(bf16[4,1,32,2,512]{4,2,3,1,0:T(8,128)(2,1)S(1)} %get-tuple-element.141), channel_id=1, source_target_pairs={{0,1},{1,2},{2,3},{4,5},{5,6},{6,7},{8,9},{9,10},{10,11},{12,13},{... | collective-permute-start | bytes 786440 | tf_op jit(solution)/shard_map/ppermute | solution.py:21
  384.8 8.7 %collective-permute-start.5 = (bf16[4,1,32,2,512]{4,2,3,1,0:T(8,128)(2,1)S(1)}, bf16[4,1,32,2,512]{4,2,3,1,0:T(8,128)(2,1)S(1)}, u32[]{:S(2)}, u32[]{:S(2)}) collective-permute-start(bf16[4,1,32,2,512]{4,2,3,1,0:T(8,128)(2,1)S(1)} %get-tuple-element.142), channel_id=1, source_target_pairs={{1,0},{2,1},{3,2},{5,4},{6,5},{7,6},{9,8},{10,9},{11,10},{13,12},{... | collective-permute-start | bytes 786440 | tf_op jit(solution)/shard_map/ppermute | solution.py:23
  386.9 8.4 %slice-start = ((s8[9437184]{0:T(1024)(128)(4,1)}), s8[4194304]{0:T(1024)(128)(4,1)S(1)}, s32[]{:S(2)}) async-start(s8[9437184]{0:T(1024)(128)(4,1)} %bitcast.214), calls=%async_computation.2 | async-start | bytes 8388608
  386.9 8.4 %slice-start.1 = ((s8[9437184]{0:T(1024)(128)(4,1)}), s8[4194304]{0:T(1024)(128)(4,1)S(1)}, s32[]{:S(2)}) async-start(s8[9437184]{0:T(1024)(128)(4,1)} %bitcast.214), calls=%async_computation.3 | async-start | bytes 8388608
  389.6 5.8 %slice-start.2 = ((s8[9437184]{0:T(1024)(128)(4,1)}), s8[1048576]{0:T(1024)(128)(4,1)S(1)}, s32[]{:S(2)}) async-start(s8[9437184]{0:T(1024)(128)(4,1)} %bitcast.214), calls=%async_computation.4 | async-start | bytes 2097152
  401.7 2.6 copy-start.3
  401.7 2.6 copy-start.7
Sparse Core Ops, SparseCore 0:
  8.9 165.1 all-gather.5
  175.6 164.9 all-gather.3
